TPU v7x, 32 devices: a whole 2x2x4 slice. The times are simulated.
32 devices in a mesh: seq: 8 (over z, x), tp: 4 (over y, core).
Axes of the slice: x: 2, y: 2, z: 4, core: 2. Of those that a mesh axis runs over, the one named last changes fastest.
Arguments:
- draft_q: bfloat16 [256, 4096], P('seq', 'tp'), may hold values from -16 to 16
- draft_kv: bfloat16 [2, 256, 4096], P(None, 'seq', 'tp'), may hold values from -6 to 6
- kv_pool: bfloat16 [2, 128, 128, 4096], P(None, 'seq', None, 'tp'), may hold values from -8 to 8
- page_table: int32 [4, 32], replicated, may hold values from -1 to 127, as said below
- cache_len: int32 [4], replicated, may hold values from 2048 to 4096, as said below
- tree_mask: int32 [4, 64, 64], replicated, may hold values from 0 to 1, as said below
- accepted_rows: int32 [4, 64], replicated, may hold values from -1 to 63, as said below
- out_weight: bfloat16 [4096, 4096], P('tp'), may hold values from -0.125 to 0.125
Outputs:
- layer_out: bfloat16 [256, 4096], P('seq', 'tp')
- accepted_kv: bfloat16 [2, 4, 128, 4096], P(None, None, None, 'tp')
Inputs may be any that keep to these rules, and one draw needn't show every extreme that they name: `page_table`: entries past a request's cached pages are -1; the slots in use are distinct over all requests. `cache_len`: some request holds exactly 4096 cached tokens. `tree_mask`: entry (r, i, k) is 1 where draft row k is row i itself or one of its ancestors in request r's token tree; a parent precedes its children, row 0 is the root. `accepted_rows`: each row lists in ascending order the draft rows of one root-to-node path of the tree, then -1.
All inputs are finite; a program needn't handle non-finite values.
Results may differ from a plain program's by a relative error of at most 0.0051.
Values may be sent and summed in bfloat16 or wider, within the bound.
A program may use at most 128 MiB of HBM per device.

v0:
```python
import math
import jax
import jax.numpy as jnp
from jax import lax
from jax.sharding import PartitionSpec as P

HD = 128
NEGATIVE = -1e30


def body(draft_q, draft_kv, kv_pool, page_table, cache_len, tree_mask, accepted_rows, out_weight):
    inv_root = 1.0 / math.sqrt(HD)
    highest = lax.Precision.HIGHEST
    n_seq = lax.axis_size("seq")
    rows_dev = draft_q.shape[0]
    width_loc = draft_q.shape[1]
    heads_loc = width_loc // HD
    n_req = page_table.shape[0]
    n_pages = page_table.shape[1]
    n_draft = tree_mask.shape[1]
    n_slots = kv_pool.shape[1]
    page_len = kv_pool.shape[2]
    rows_all = rows_dev * n_seq
    query_all, kv_all = (
        lax.all_gather(draft_q, "seq", axis=0, tiled=True),
        lax.all_gather(draft_kv, "seq", axis=1, tiled=True),
    )
    first_slot = lax.axis_index("seq") * n_slots
    slot_ids = first_slot + jnp.arange(n_slots, dtype=jnp.int32)
    slot_hits = page_table[None, :, :] == slot_ids[:, None, None]
    owner_hot = jnp.any(slot_hits, axis=2)
    is_live = jnp.any(owner_hot, axis=1)
    owner_req = jnp.sum(owner_hot * jnp.arange(n_req, dtype=jnp.int32)[None, :], axis=1)
    logical = jnp.sum(slot_hits * jnp.arange(n_pages, dtype=jnp.int32)[None, None, :], axis=(1, 2))
    len_limit = jnp.sum(owner_hot * cache_len[None, :], axis=1)
    positions = logical[:, None] * page_len + jnp.arange(page_len, dtype=jnp.int32)[None, :]
    is_valid = is_live[:, None] & (positions < len_limit[:, None])
    query_req = query_all.reshape(n_req, n_draft, heads_loc, HD)
    page_query = query_req[owner_req]
    page_keys = kv_pool[0].reshape(n_slots, page_len, heads_loc, HD)
    page_values = kv_pool[1].reshape(n_slots, page_len, heads_loc, HD)
    scores = (
        jnp.einsum("sqhd,sthd->shqt", page_query, page_keys, preferred_element_type=jnp.float32)
        * inv_root
    )
    allowed = is_valid[:, None, None, :]
    masked = jnp.where(allowed, scores, NEGATIVE)
    page_max = jnp.max(masked, axis=3)
    weights = jnp.where(allowed, jnp.exp(masked - page_max[..., None]), 0.0)
    page_total = jnp.sum(weights, axis=3)
    page_out = jnp.einsum(
        "shqt,sthd->shqd",
        weights.astype(jnp.bfloat16),
        page_values,
        preferred_element_type=jnp.float32,
    )
    req_max = jnp.max(
        jnp.where(owner_hot[:, :, None, None], page_max[:, None, :, :], NEGATIVE), axis=0
    )
    weight = jnp.exp(page_max - req_max[owner_req])
    own_hot = owner_hot.astype(jnp.float32)
    local_total = jnp.einsum(
        "sr,shq->rqh", own_hot, weight * page_total, precision=highest
    ).reshape(rows_all, heads_loc)
    local_out = jnp.einsum(
        "sr,shqd->rqhd", own_hot, weight[..., None] * page_out, precision=highest
    ).reshape(rows_all, width_loc)
    local_max = jnp.transpose(req_max, (0, 2, 1)).reshape(rows_all, heads_loc)
    row_start = lax.axis_index("seq") * rows_dev
    got_max, got_total, got_out = (
        lax.all_to_all(local_max, "seq", split_axis=0, concat_axis=0, tiled=True),
        lax.all_to_all(local_total, "seq", split_axis=0, concat_axis=0, tiled=True),
        lax.all_to_all(local_out, "seq", split_axis=0, concat_axis=0, tiled=True),
    )
    got_max = got_max.reshape(n_seq, rows_dev, heads_loc)
    own_max = jnp.max(got_max, axis=0)
    factor = jnp.exp(got_max - own_max[None])
    own_total = jnp.sum(got_total.reshape(n_seq, rows_dev, heads_loc) * factor, axis=0)
    own_out = jnp.sum(got_out.reshape(n_seq, rows_dev, heads_loc, HD) * factor[..., None], axis=0)
    own_query = draft_q.reshape(rows_dev, heads_loc, HD)
    tree_keys = kv_all[0].reshape(rows_all, heads_loc, HD)
    tree_values = kv_all[1].reshape(rows_all, heads_loc, HD)
    ancestry = tree_mask.reshape(rows_all, n_draft)
    own_ancestry = lax.dynamic_slice_in_dim(ancestry, row_start, rows_dev, 0)
    row_req = (row_start + jnp.arange(rows_dev, dtype=jnp.int32)) // n_draft
    key_req = jnp.arange(rows_all, dtype=jnp.int32) // n_draft
    tree_allowed = (jnp.tile(own_ancestry, (1, n_req)) == 1) & (
        row_req[:, None] == key_req[None, :]
    )
    tree_scores = (
        jnp.einsum("qhd,khd->hqk", own_query, tree_keys, preferred_element_type=jnp.float32)
        * inv_root
    )
    tree_masked = jnp.where(tree_allowed[None], tree_scores, NEGATIVE)
    tree_max = jnp.max(tree_masked, axis=2)
    tree_weights = jnp.where(tree_allowed[None], jnp.exp(tree_masked - tree_max[..., None]), 0.0)
    tree_total = jnp.transpose(jnp.sum(tree_weights, axis=2))
    tree_out = jnp.einsum(
        "hqk,khd->qhd",
        tree_weights.astype(jnp.bfloat16),
        tree_values,
        preferred_element_type=jnp.float32,
    )
    tree_max = jnp.transpose(tree_max)
    row_top = jnp.maximum(own_max, tree_max)
    cache_factor = jnp.exp(own_max - row_top)
    tree_factor = jnp.exp(tree_max - row_top)
    numerator = own_out * cache_factor[..., None] + tree_out * tree_factor[..., None]
    denominator = own_total * cache_factor + tree_total * tree_factor
    attention = (
        (numerator / denominator[..., None]).reshape(rows_dev, width_loc).astype(jnp.bfloat16)
    )
    partial_value = jnp.dot(attention, out_weight, preferred_element_type=jnp.float32)
    layer_out = lax.psum_scatter(partial_value, "tp", scatter_dimension=1, tiled=True).astype(
        jnp.bfloat16
    )
    picked = jnp.concatenate(
        [accepted_rows, jnp.full((n_req, page_len - n_draft), -1, jnp.int32)], axis=1
    )
    onehot = (picked[:, :, None] == jnp.arange(n_draft, dtype=jnp.int32)[None, None, :]).astype(
        jnp.bfloat16
    )
    kv_blocks = kv_all.reshape(2, n_req, n_draft, width_loc)
    accepted_kv = jnp.einsum(
        "rji,crid->crjd", onehot, kv_blocks, preferred_element_type=jnp.float32
    ).astype(jnp.bfloat16)
    return (layer_out, accepted_kv)


def solution(mesh):
    return jax.shard_map(
        body,
        mesh=mesh,
        in_specs=(
            P("seq", "tp"),
            P(None, "seq", "tp"),
            P(None, "seq", None, "tp"),
            P(),
            P(),
            P(),
            P(),
            P("tp", None),
        ),
        out_specs=(P("seq", "tp"), P(None, None, None, "tp")),
        check_vma=False,
    )
```

profile of v0, /device:TPU:0, one launch (start us, length us, event | category | flops | bytes accessed | tf_op | source)
XLA Modules:
  0.0 172.4 jit_solution(13782191911061992662)
XLA Ops:
  7.2 1.0 compare_reduce_fusion.1
  8.2 0.9 fusion.38
  9.2 0.7 select_reduce_fusion.2
  9.9 33.2 %all_gather.6 = bf16[256,1024]{1,0:T(8,128)(2,1)S(1)} all-gather(bf16[32,1024]{1,0:T(8,128)(2,1)} %param.8), channel_id=1, replica_groups=mesh['seq'=8,'tp'=4] {'seq'}, dimensions={0}, use_global_device_ids=true | all-gather | bytes 589824 | tf_op jit(solution)/shard_map/all_gather | solution.py:25
  43.2 6.0 %fusion.53 = (bf16[1,16,128,1024]{3,2,1,0:T(8,128)(2,1)}, bf16[1,16,128,1024]{3,2,1,0:T(8,128)(2,1)}) fusion(bf16[2,16,128,1024]{3,2,1,0:T(8,128)(2,1)} %param.10), kind=kLoop, calls=%fused_computation.86 | loop fusion | bytes 16777216 | tf_op jit(solution)/shard_map/slice | solution.py:40
  49.3 6.4 %copy.128 = bf16[1,16,128,1024]{2,3,1,0:T(8,128)(2,1)} copy(bf16[1,16,128,1024]{3,2,1,0:T(8,128)(2,1)} %get-tuple-element.25) | data formatting | bytes 8388608
  55.6 0.9 gather_fusion
  56.7 3.5 %fusion.2 = (f32[16,8,64]{2,1,0:T(8,128)S(1)}, f32[16,8,64,128]{3,2,1,0:T(8,128)S(1)}) fusion(pred[16,128]{1,0:T(8,128)(4,1)S(1)} %fusion.39, bf16[16,128,8,128]{1,3,2,0:T(8,128)(2,1)} %bitcast.99, bf16[16,64,8,128]{3,2,1,0:T(8,128)(2,1)S(1)} %gather_fusion), kind=kOutput, calls=%fused_computation.6 | convolution fusion | flops 271572992 | bytes 10520576 | tf_op jit(solution)/shard_map/sqhd,sthd->shqt/dot_general | solution.py:43
  60.2 1.9 %copy-done = f32[16,8,64,128]{3,2,1,0:T(8,128)} copy-done((f32[16,8,64,128]{3,2,1,0:T(8,128)}, f32[16,8,64,128]{3,2,1,0:T(8,128)S(1)}, u32[]{:S(2)}) %copy-start) | copy-done | bytes 4194328
  62.1 2.4 %fusion.3 = f32[16,8,64]{2,1,0:T(8,128)S(1)} fusion(f32[16,8,64,128]{3,2,1,0:T(8,128)S(1)} %get-tuple-element.30, f32[16,8,64]{2,1,0:T(8,128)S(1)} %get-tuple-element.29, pred[16,128]{1,0:T(8,128)(4,1)S(1)} %fusion.39), kind=kLoop, calls=%fused_computation.7 | loop fusion | flops 5234688 | bytes 4261888 | tf_op jit(solution)/shard_map/reduce_sum | solution.py:50
  65.6 0.7 reshape.220
  66.2 5.7 %all-to-all-start.2 = ((f32[8,1,256]{2,1,0:T(1,128)}), f32[8,1,256]{2,1,0:T(1,128)S(1)}, u32[]{:S(2)}, u32[]{:S(2)}) async-start(f32[8,1,256]{2,1,0:T(1,128)} %reshape.220), calls=%async_computation.2 | async-start | bytes 16384 | tf_op jit(solution)/shard_map/all_to_all | solution.py:72
  71.9 0.8 copy.107
  72.8 6.4 %copy.129 = bf16[1,16,128,1024]{2,3,1,0:T(8,128)(2,1)} copy(bf16[1,16,128,1024]{3,2,1,0:T(8,128)(2,1)} %get-tuple-element.26) | data formatting | bytes 8388608
  79.1 6.6 %convolution_multiply_fusion = f32[16,8,64,128]{3,2,1,0:T(8,128)} fusion(bf16[16,128,8,128]{1,3,2,0:T(8,128)(2,1)} %bitcast.100, f32[16,8,64,128]{3,2,1,0:T(8,128)} %copy-done, f32[16,8,64]{2,1,0:T(8,128)S(1)} %get-tuple-element.29, f32[16,8,64]{2,1,0:T(8,128)S(1)} %get-tuple-element.24, pred[16,128]{1,0:T(8,128)(4,1)S(1)} %fusion.39), kind=kOutput, calls=%fused_computation.9 | convolution fusion | flops 274726912 | bytes 12650496 | tf_op jit(solution)/shard_map/shqt,sthd->shqd/dot_general | solution.py:51
  85.9 0.7 reshape.218
  86.6 6.0 %all-to-all-start.1 = ((f32[8,1,256]{2,1,0:T(1,128)}), f32[8,1,256]{2,1,0:T(1,128)S(1)}, u32[]{:S(2)}, u32[]{:S(2)}) async-start(f32[8,1,256]{2,1,0:T(1,128)} %reshape.218), calls=%async_computation.1 | async-start | bytes 16384 | tf_op jit(solution)/shard_map/all_to_all | solution.py:71
  92.5 5.9 %fusion.13 = f32[4,64,8,128]{3,0,1,2:T(4,128)S(1)} fusion(f32[16,8,64,128]{3,2,1,0:T(8,128)} %convolution_multiply_fusion, pred[16,4]{0,1:T(4,128)(4,1)S(1)} %get-tuple-element.15), kind=kOutput, calls=%fused_computation.18 | convolution fusion | flops 50331648 | bytes 5242944 | tf_op jit(solution)/shard_map/sr,shqd->rqhd/dot_general | solution.py:65
  99.1 1.1 all_to_all.18
  100.2 6.0 %all-to-all-start = ((f32[8,32,1024]{2,1,0:T(8,128)}), f32[8,32,1024]{2,1,0:T(8,128)S(1)}, u32[]{:S(2)}, u32[]{:S(2)}) async-start(f32[8,32,1024]{2,1,0:T(8,128)} %all_to_all.18), calls=%async_computation | async-start | bytes 2097152 | tf_op jit(solution)/shard_map/all_to_all | solution.py:73
  106.4 0.7 dynamic-slice_compare_fusion
  110.0 13.2 %all-gather.2.cloned.1.call-done = bf16[2,256,1024]{2,0,1:T(2,128)(2,1)} async-done(((bf16[2,32,1024]{2,0,1:T(2,128)(2,1)}), bf16[2,256,1024]{2,0,1:T(2,128)(2,1)}) %all-gather.2.cloned.1.call-update) | async-done | bytes 1048592 | tf_op jit(solution)/shard_map/all_gather | solution.py:26
  123.2 4.1 %fusion.54 = (bf16[1,256,1024]{2,0,1:T(2,128)(2,1)}, bf16[1,256,1024]{2,0,1:T(2,128)(2,1)S(1)}) fusion(bf16[2,256,1024]{2,0,1:T(2,128)(2,1)} %all-gather.2.cloned.1.call-done), kind=kLoop, calls=%fused_computation.87 | loop fusion | bytes 2097152 | tf_op jit(solution)/shard_map/slice | solution.py:81
  127.3 3.5 %copy.130 = bf16[1,256,1024]{1,2,0:T(8,128)(2,1)} copy(bf16[1,256,1024]{2,0,1:T(2,128)(2,1)} %get-tuple-element.27) | data formatting | bytes 1048576
  130.8 2.0 %copy.131 = bf16[1,256,1024]{1,2,0:T(8,128)(2,1)} copy(bf16[1,256,1024]{2,0,1:T(2,128)(2,1)S(1)} %get-tuple-element.28) | data formatting | bytes 1048576
  132.8 1.3 fusion.55
  134.5 1.4 fusion.21
  135.9 5.8 %fusion.31 = f32[32,4096]{1,0:T(8,128)} fusion(bf16[1024,4096]{1,0:T(8,128)(2,1)} %param.15, bf16[8,4,8,128]{3,2,1,0:T(8,128)(2,1)S(1)} %fusion.21), kind=kOutput, calls=%fused_computation.40 | convolution fusion | flops 268435456 | bytes 8978432 | tf_op jit(solution)/shard_map/dot_general | solution.py:113
  141.8 0.8 convert_bitcast_fusion
  142.6 1.5 copy.119
  144.0 20.0 %reduce-scatter.2.cloned.1.call-done = f32[32,1024]{1,0:T(8,128)} async-done(((f32[32,4096]{1,0:T(8,128)}), f32[32,1024]{1,0:T(8,128)}) %reduce-scatter.2.cloned.1.call-update) | async-done | bytes 131088 | tf_op jit(solution)/shard_map/reduce_scatter | solution.py:114
  164.0 1.5 convert_element_type.30
  (52 shorter events, 5.5 us)
Async XLA Ops:
  60.2 2.0 %copy-start = (f32[16,8,64,128]{3,2,1,0:T(8,128)}, f32[16,8,64,128]{3,2,1,0:T(8,128)S(1)}, u32[]{:S(2)}) copy-start(f32[16,8,64,128]{3,2,1,0:T(8,128)S(1)} %get-tuple-element.30) | copy-start | bytes 12582916
  60.2 11.8 %copy-start.3 = (bf16[2,32,1024]{2,1,0:T(8,128)(2,1)S(1)}, bf16[2,32,1024]{2,1,0:T(8,128)(2,1)}, u32[]{:S(2)}) copy-start(bf16[2,32,1024]{2,1,0:T(8,128)(2,1)} %param.9) | copy-start | bytes 393220
  66.2 20.3 %all-to-all-start.2 = ((f32[8,1,256]{2,1,0:T(1,128)}), f32[8,1,256]{2,1,0:T(1,128)S(1)}, u32[]{:S(2)}, u32[]{:S(2)}) async-start(f32[8,1,256]{2,1,0:T(1,128)} %reshape.220), calls=%async_computation.2 | async-start | bytes 16384 | tf_op jit(solution)/shard_map/all_to_all | solution.py:72
  71.9 51.4 %all-gather.2.cloned.1.call-start = ((), (), s32[]{:S(2)}) async-start(), calls=%async_computation.4 | async-start | bytes 1179648 | tf_op jit(solution)/shard_map/all_gather | solution.py:26
  86.6 13.7 %all-to-all-start.1 = ((f32[8,1,256]{2,1,0:T(1,128)}), f32[8,1,256]{2,1,0:T(1,128)S(1)}, u32[]{:S(2)}, u32[]{:S(2)}) async-start(f32[8,1,256]{2,1,0:T(1,128)} %reshape.218), calls=%async_computation.1 | async-start | bytes 16384 | tf_op jit(solution)/shard_map/all_to_all | solution.py:71
  100.2 34.1 %all-to-all-start = ((f32[8,32,1024]{2,1,0:T(8,128)}), f32[8,32,1024]{2,1,0:T(8,128)S(1)}, u32[]{:S(2)}, u32[]{:S(2)}) async-start(f32[8,32,1024]{2,1,0:T(8,128)} %all_to_all.18), calls=%async_computation | async-start | bytes 2097152 | tf_op jit(solution)/shard_map/all_to_all | solution.py:73
  106.2 57.8 %reduce-scatter.2.cloned.1.call-start = ((), (), s32[]{:S(2)}) async-start(), calls=%async_computation.5 | async-start | bytes 655360 | tf_op jit(solution)/shard_map/reduce_scatter | solution.py:114
  110.0 22.8 %copy-start.2 = (bf16[32,1024]{1,0:T(8,128)(2,1)S(1)}, bf16[32,1024]{1,0:T(8,128)(2,1)}, u32[]{:S(2)}) copy-start(bf16[32,1024]{1,0:T(8,128)(2,1)} %param.8) | copy-start | bytes 196612
  135.9 5.9 %copy-start.4 = (s32[4,64]{1,0:T(4,128)S(1)}, s32[4,64]{1,0:T(4,128)}, u32[]{:S(2)}) copy-start(s32[4,64]{1,0:T(4,128)} %param.14) | copy-start | bytes 3076
  135.9 5.9 %copy-start.1 = (bf16[2,256,1024]{2,0,1:T(2,128)(2,1)S(1)}, bf16[2,256,1024]{2,0,1:T(2,128)(2,1)}, u32[]{:S(2)}) copy-start(bf16[2,256,1024]{2,0,1:T(2,128)(2,1)} %all-gather.2.cloned.1.call-done) | copy-start | bytes 3145732
Sparse Core Ops, SparseCore 0:
  75.4 47.7 all-gather.1
  141.9 22.0 reduce-scatter.1
where the time goes:
time: 173 us; the launch traced here: 172 us
  local copies, waits for them, and re-layouts  38.9 us (22%)
  blocking collectives  33.2 us (19%)
  waiting for transfers between devices  33.2 us (19%)
  matrix products  25.5 us (15%)
  starting transfers between devices  17.8 us (10%)
  between operations  14.3 us (8%)
  other arithmetic  9.37 us (5%)
    all_gather x1, blocking collectives, body(): lax.all_gather(draft_q, 'seq', axis=0, tiled=True)  33.2 us
    unnamed x21, local copies, waits for them, and re-layouts  24 us
    reduce_scatter x1, waiting for transfers between devices, body(): lax.psum_scatter(partial_value, 'tp', scatter_dimension=1, tiled=True)  20 us
    all_gather x1, waiting for transfers between devices, body(): lax.all_gather(draft_kv, 'seq', axis=1, tiled=True)  13.2 us
    dot_general x1, matrix products, body(): jnp.einsum('shqt,sthd->shqd', weights.astype(jnp.bfloat16), page_values,...  6.64 us
    slice x1, local copies, waits for them, and re-layouts, body(): page_keys = kv_pool[0].reshape(n_slots, page_len, heads_loc, HD)  6.01 us
    all_to_all x1, starting transfers between devices, body(): lax.all_to_all(local_out, 'seq', split_axis=0, concat_axis=0, tiled=True)  5.98 us
    all_to_all x1, starting transfers between devices, body(): lax.all_to_all(local_max, 'seq', split_axis=0, concat_axis=0, tiled=True)  5.95 us
  transfers between devices with their start and end apart: 5, of which 2 were waited for; matrix products, arithmetic and copies ran while one was open for 22% of the time, Pallas kernels for 0%

commit v1 on v0

--- a/solution.py
+++ b/solution.py
@@ -6,6 +6,39 @@
 
 HD = 128
 NEGATIVE = -1e30
+
+
+def apply_page_all(xx, which_dim):
+    main = list(xx.shape[1:])
+    main[which_dim] *= xx.shape[0]
+    out_arr = jnp.moveaxis(xx, 0, which_dim).reshape(main)
+    return out_arr
+
+
+def _draw_floor(inp, axis_id):
+    h_now = lax.axis_size(axis_id)
+    z_new = lax.axis_index(axis_id)
+    f_now, view_out = (h_now, z_new)
+    g_now, work_now = (inp[None], 1)
+    while work_now < f_now:
+        panels = []
+        s = 0
+        while s < f_now:
+            panels.append((s, s ^ work_now))
+            s += 1
+        answer = lax.ppermute(g_now, axis_id, panels)
+        local_now = view_out & work_now == 0
+        back = jnp.where(local_now, g_now, answer)
+        x_new = jnp.where(local_now, answer, g_now)
+        g_now = jnp.concatenate([back, x_new])
+        work_now *= 2
+    return g_now
+
+
+def deliver_the_counts(z, xs, dim_at):
+    current_value = _draw_floor(z, xs)
+    placed = apply_page_all(current_value, dim_at)
+    return placed
 
 
 def body(draft_q, draft_kv, kv_pool, page_table, cache_len, tree_mask, accepted_rows, out_weight):
@@ -22,7 +55,7 @@
     page_len = kv_pool.shape[2]
     rows_all = rows_dev * n_seq
     query_all, kv_all = (
-        lax.all_gather(draft_q, "seq", axis=0, tiled=True),
+        deliver_the_counts(draft_q, "seq", 0),
         lax.all_gather(draft_kv, "seq", axis=1, tiled=True),
     )
     first_slot = lax.axis_index("seq") * n_slots

time: 173 us -> 147 us (0.85)
  blocking collectives: 33.2 us -> 0 us
  starting transfers between devices: 17.8 us -> 23.3 us
    all_gather x1 -> x0, blocking collectives: 33.2 us -> none  [body(): lax.all_gather(draft_q, 'seq', axis=0, tiled=True)]
    all_gather x1, waiting for transfers between devices: 13.2 us -> 0.02 us  [body(): lax.all_gather(draft_kv, 'seq', axis=1, tiled=True)]
    all_to_all x1, waiting for transfers between devices: 0.01 us -> 10.1 us  [body(): lax.all_to_all(local_out, 'seq', split_axis=0, concat_axis=0, tiled=True)]
    ppermute x0 -> x3, starting transfers between devices: none -> 7.27 us  [_draw_floor(): answer = lax.ppermute(g_now, axis_id, panels)]
    ppermute x0 -> x3, waiting for transfers between devices: none -> 5.3 us  [_draw_floor(): answer = lax.ppermute(g_now, axis_id, panels)]
    all_to_all x1, starting transfers between devices: 5.66 us -> 3.75 us  [body(): lax.all_to_all(local_total, 'seq', split_axis=0, concat_axis=0, tiled=True)]
  transfers between devices with their start and end apart: 5 -> 8, of which waited for: 2 -> 4; matrix products, arithmetic and copies ran while one was open for 22% -> 43% of each run, Pallas kernels for 0% -> 0%
where the time goes in v1:
time: 147 us; the launch traced here: 146 us
  local copies, waits for them, and re-layouts  39.9 us (27%)
  waiting for transfers between devices  33.9 us (23%)
  matrix products  25.5 us (17%)
  starting transfers between devices  23.3 us (16%)
  between operations  14.4 us (10%)
  other arithmetic  8.86 us (6%)
    unnamed x21, local copies, waits for them, and re-layouts  25 us
    reduce_scatter x1, waiting for transfers between devices, body(): lax.psum_scatter(partial_value, 'tp', scatter_dimension=1, tiled=True)  18.5 us
    all_to_all x1, waiting for transfers between devices, body(): lax.all_to_all(local_out, 'seq', split_axis=0, concat_axis=0, tiled=True)  10.1 us
    ppermute x3, starting transfers between devices, _draw_floor(): answer = lax.ppermute(g_now, axis_id, panels)  7.27 us
    dot_general x1, matrix products, body(): jnp.einsum('shqt,sthd->shqd', weights.astype(jnp.bfloat16), page_values,...  6.65 us
    slice x1, local copies, waits for them, and re-layouts, body(): page_keys = kv_pool[0].reshape(n_slots, page_len, heads_loc, HD)  6.09 us
    all_to_all x1, starting transfers between devices, body(): lax.all_to_all(local_out, 'seq', split_axis=0, concat_axis=0, tiled=True)  6 us
    all_to_all x1, starting transfers between devices, body(): lax.all_to_all(local_max, 'seq', split_axis=0, concat_axis=0, tiled=True)  5.99 us
  transfers between devices with their start and end apart: 8, of which 4 were waited for; matrix products, arithmetic and copies ran while one was open for 43% of the time, Pallas kernels for 0%

profile of v1, /device:TPU:0, one launch (start us, length us, event | category | flops | bytes accessed | tf_op | source)
XLA Modules:
  0.0 145.8 jit_solution(12775370423795322277)
XLA Ops:
  7.2 3.0 %collective-permute-start = (bf16[1,32,1024]{2,1,0:T(8,128)(2,1)}, bf16[1,32,1024]{2,1,0:T(8,128)(2,1)S(1)}, u32[]{:S(2)}, u32[]{:S(2)}) collective-permute-start(bf16[1,32,1024]{2,1,0:T(8,128)(2,1)} %bitcast.111), channel_id=1, source_target_pairs={{0,4},{4,0},{8,12},{12,8},{16,20},{20,16},{24,28},{28,24},{1,5},{5... | collective-permute-start | bytes 196616 | tf_op jit(solution)/shard_map/ppermute | solution.py:29
  10.2 1.7 %copy.107 = bf16[2,32,1024]{2,0,1:T(2,128)(2,1)} copy(bf16[2,32,1024]{2,1,0:T(8,128)(2,1)} %param.9) | data formatting | bytes 262144 | tf_op args[1]
  12.0 1.0 compare_reduce_fusion.1
  13.0 0.7 select_reduce_fusion.2
  13.7 6.1 %fusion.53 = (bf16[1,16,128,1024]{3,2,1,0:T(8,128)(2,1)}, bf16[1,16,128,1024]{3,2,1,0:T(8,128)(2,1)}) fusion(bf16[2,16,128,1024]{3,2,1,0:T(8,128)(2,1)} %param.10), kind=kLoop, calls=%fused_computation.95 | loop fusion | bytes 16777216 | tf_op jit(solution)/shard_map/slice | solution.py:73
  20.1 1.6 %collective-permute-start.1 = (bf16[2,32,1024]{2,1,0:T(8,128)(2,1)S(1)}, bf16[2,32,1024]{2,1,0:T(8,128)(2,1)S(1)}, u32[]{:S(2)}, u32[]{:S(2)}) collective-permute-start(bf16[2,32,1024]{2,1,0:T(8,128)(2,1)S(1)} %pad_maximum_fusion.2), channel_id=1, source_target_pairs={{0,8},{4,12},{8,0},{12,4},{16,24},{20,28},{24,16},{28,20},{1,9},{5... | collective-permute-start | bytes 393224 | tf_op jit(solution)/shard_map/ppermute | solution.py:29
  21.7 4.8 %collective-permute-done.1 = bf16[2,32,1024]{2,1,0:T(8,128)(2,1)S(1)} collective-permute-done((bf16[2,32,1024]{2,1,0:T(8,128)(2,1)S(1)}, bf16[2,32,1024]{2,1,0:T(8,128)(2,1)S(1)}, u32[]{:S(2)}, u32[]{:S(2)}) %collective-permute-start.1) | collective-permute-done | bytes 131104 | tf_op jit(solution)/shard_map/ppermute | solution.py:29
  26.6 2.6 %collective-permute-start.2 = (bf16[4,32,1024]{2,1,0:T(8,128)(2,1)S(1)}, bf16[4,32,1024]{2,1,0:T(8,128)(2,1)S(1)}, u32[]{:S(2)}, u32[]{:S(2)}) collective-permute-start(bf16[4,32,1024]{2,1,0:T(8,128)(2,1)S(1)} %pad_maximum_fusion.1), channel_id=1, source_target_pairs={{0,16},{4,20},{8,24},{12,28},{16,0},{20,4},{24,8},{28,12},{1,17},{... | collective-permute-start | bytes 786440 | tf_op jit(solution)/shard_map/ppermute | solution.py:29
  29.3 6.4 %copy.128 = bf16[1,16,128,1024]{2,3,1,0:T(8,128)(2,1)} copy(bf16[1,16,128,1024]{3,2,1,0:T(8,128)(2,1)} %get-tuple-element.25) | data formatting | bytes 8388608
  35.7 6.4 %copy.129 = bf16[1,16,128,1024]{2,3,1,0:T(8,128)(2,1)} copy(bf16[1,16,128,1024]{3,2,1,0:T(8,128)(2,1)} %get-tuple-element.26) | data formatting | bytes 8388608
  42.8 1.0 gather_fusion
  43.8 3.5 %fusion.2 = (f32[16,8,64]{2,1,0:T(8,128)S(1)}, f32[16,8,64,128]{3,2,1,0:T(8,128)S(1)}) fusion(pred[16,128]{1,0:T(8,128)(4,1)S(1)} %fusion.39, bf16[16,128,8,128]{1,3,2,0:T(8,128)(2,1)} %bitcast.104, bf16[16,64,8,128]{3,2,1,0:T(8,128)(2,1)S(1)} %gather_fusion), kind=kOutput, calls=%fused_computation.6 | convolution fusion | flops 271572992 | bytes 10520576 | tf_op jit(solution)/shard_map/sqhd,sthd->shqt/dot_general | solution.py:76
  47.3 2.0 %copy-done = f32[16,8,64,128]{3,2,1,0:T(8,128)} copy-done((f32[16,8,64,128]{3,2,1,0:T(8,128)}, f32[16,8,64,128]{3,2,1,0:T(8,128)S(1)}, u32[]{:S(2)}) %copy-start) | copy-done | bytes 4194328
  49.3 2.4 %fusion.3 = f32[16,8,64]{2,1,0:T(8,128)S(1)} fusion(f32[16,8,64,128]{3,2,1,0:T(8,128)S(1)} %get-tuple-element.36, f32[16,8,64]{2,1,0:T(8,128)S(1)} %get-tuple-element.35, pred[16,128]{1,0:T(8,128)(4,1)S(1)} %fusion.39), kind=kLoop, calls=%fused_computation.7 | loop fusion | flops 5234688 | bytes 4261888 | tf_op jit(solution)/shard_map/reduce_sum | solution.py:83
  53.4 3.8 %all-to-all-start.2 = ((f32[8,1,256]{2,1,0:T(1,128)}), f32[8,1,256]{2,1,0:T(1,128)S(1)}, u32[]{:S(2)}, u32[]{:S(2)}) async-start(f32[8,1,256]{2,1,0:T(1,128)} %reshape.216), calls=%async_computation.2 | async-start | bytes 16384 | tf_op jit(solution)/shard_map/all_to_all | solution.py:105
  57.1 6.6 %convolution_multiply_fusion = f32[16,8,64,128]{3,2,1,0:T(8,128)} fusion(bf16[16,128,8,128]{1,3,2,0:T(8,128)(2,1)} %bitcast.103, f32[16,8,64,128]{3,2,1,0:T(8,128)} %copy-done, f32[16,8,64]{2,1,0:T(8,128)S(1)} %get-tuple-element.35, f32[16,8,64]{2,1,0:T(8,128)S(1)} %get-tuple-element.24, pred[16,128]{1,0:T(8,128)(4,1)S(1)} %fusion.39), kind=kOutput, calls=%fused_computation.9 | convolution fusion | flops 274726912 | bytes 12650496 | tf_op jit(solution)/shard_map/shqt,sthd->shqd/dot_general | solution.py:84
  64.5 6.0 %all-to-all-start.1 = ((f32[8,1,256]{2,1,0:T(1,128)}), f32[8,1,256]{2,1,0:T(1,128)S(1)}, u32[]{:S(2)}, u32[]{:S(2)}) async-start(f32[8,1,256]{2,1,0:T(1,128)} %reshape.214), calls=%async_computation.1 | async-start | bytes 16384 | tf_op jit(solution)/shard_map/all_to_all | solution.py:104
  70.5 5.9 %fusion.13 = f32[4,64,8,128]{3,0,1,2:T(4,128)S(1)} fusion(f32[16,8,64,128]{3,2,1,0:T(8,128)} %convolution_multiply_fusion, pred[16,4]{0,1:T(4,128)(4,1)S(1)} %get-tuple-element.15), kind=kOutput, calls=%fused_computation.18 | convolution fusion | flops 50331648 | bytes 5242944 | tf_op jit(solution)/shard_map/sr,shqd->rqhd/dot_general | solution.py:98
  77.1 1.1 all_to_all.18
  78.2 6.0 %all-to-all-start = ((f32[8,32,1024]{2,1,0:T(8,128)}), f32[8,32,1024]{2,1,0:T(8,128)S(1)}, u32[]{:S(2)}, u32[]{:S(2)}) async-start(f32[8,32,1024]{2,1,0:T(8,128)} %all_to_all.18), calls=%async_computation | async-start | bytes 2097152 | tf_op jit(solution)/shard_map/all_to_all | solution.py:106
  84.5 0.7 dynamic-slice_compare_fusion
  88.1 4.1 %fusion.54 = (bf16[1,256,1024]{2,0,1:T(2,128)(2,1)}, bf16[1,256,1024]{2,0,1:T(2,128)(2,1)S(1)}) fusion(bf16[2,256,1024]{2,0,1:T(2,128)(2,1)} %all-gather.2.cloned.1.call-done), kind=kLoop, calls=%fused_computation.96 | loop fusion | bytes 2097152 | tf_op jit(solution)/shard_map/slice | solution.py:114
  92.2 3.5 %copy.130 = bf16[1,256,1024]{1,2,0:T(8,128)(2,1)} copy(bf16[1,256,1024]{2,0,1:T(2,128)(2,1)} %get-tuple-element.27) | data formatting | bytes 1048576
  95.7 2.0 %copy.131 = bf16[1,256,1024]{1,2,0:T(8,128)(2,1)} copy(bf16[1,256,1024]{2,0,1:T(2,128)(2,1)S(1)} %get-tuple-element.28) | data formatting | bytes 1048576
  97.6 1.3 fusion.55
  99.2 10.1 %all-to-all-done = f32[8,32,1024]{2,1,0:T(8,128)S(1)} async-done(((f32[8,32,1024]{2,1,0:T(8,128)}), f32[8,32,1024]{2,1,0:T(8,128)S(1)}, u32[]{:S(2)}, u32[]{:S(2)}) %all-to-all-start) | async-done | bytes 1048608 | tf_op jit(solution)/shard_map/all_to_all | solution.py:106
  109.4 1.4 fusion.21
  110.9 5.8 %fusion.31 = f32[32,4096]{1,0:T(8,128)} fusion(bf16[1024,4096]{1,0:T(8,128)(2,1)} %param.15, bf16[8,4,8,128]{3,2,1,0:T(8,128)(2,1)S(1)} %fusion.21), kind=kOutput, calls=%fused_computation.47 | convolution fusion | flops 268435456 | bytes 8978432 | tf_op jit(solution)/shard_map/dot_general | solution.py:146
  116.7 0.8 convert_bitcast_fusion
  117.5 1.5 %copy.119 = bf16[2,4,128,1024]{3,2,1,0:T(8,128)(2,1)} copy(bf16[2,4,128,1024]{3,2,0,1:T(8,128)(2,1)S(1)} %convert_bitcast_fusion) | data formatting | bytes 4194304
  119.0 18.5 %reduce-scatter.2.cloned.1.call-done = f32[32,1024]{1,0:T(8,128)} async-done(((f32[32,4096]{1,0:T(8,128)}), f32[32,1024]{1,0:T(8,128)}) %reduce-scatter.2.cloned.1.call-update) | async-done | bytes 131088 | tf_op jit(solution)/shard_map/reduce_scatter | solution.py:147
  137.4 1.5 %convert_element_type.30 = bf16[32,1024]{1,0:T(8,128)(2,1)} convert(f32[32,1024]{1,0:T(8,128)} %reduce-scatter.2.cloned.1.call-done) | non-fusion elementwise | flops 32768 | bytes 196608 | tf_op jit(solution)/shard_map/convert_element_type | solution.py:147
  (63 shorter events, 7.7 us)
Async XLA Ops:
  7.2 80.9 %all-gather.2.cloned.1.call-start = ((), (), s32[]{:S(2)}) async-start(), calls=%async_computation.4 | async-start | bytes 1179648 | tf_op jit(solution)/shard_map/all_gather | solution.py:59
  7.2 12.8 %collective-permute-start = (bf16[1,32,1024]{2,1,0:T(8,128)(2,1)}, bf16[1,32,1024]{2,1,0:T(8,128)(2,1)S(1)}, u32[]{:S(2)}, u32[]{:S(2)}) collective-permute-start(bf16[1,32,1024]{2,1,0:T(8,128)(2,1)} %bitcast.111), channel_id=1, source_target_pairs={{0,4},{4,0},{8,12},{12,8},{16,20},{20,16},{24,28},{28,24},{1,5},{5... | collective-permute-start | bytes 196616 | tf_op jit(solution)/shard_map/ppermute | solution.py:29
  13.7 6.1 %copy-start.3 = (s32[4,32]{1,0:T(4,128)S(1)}, s32[4,32]{1,0:T(4,128)}, u32[]{:S(2)}) copy-start(s32[4,32]{1,0:T(4,128)} %param.11) | copy-start | bytes 1540
  13.7 6.3 %copy-start.2 = (bf16[32,1024]{1,0:T(8,128)(2,1)S(1)}, bf16[32,1024]{1,0:T(8,128)(2,1)}, u32[]{:S(2)}) copy-start(bf16[32,1024]{1,0:T(8,128)(2,1)} %param.8) | copy-start | bytes 196612
  20.1 6.5 %collective-permute-start.1 = (bf16[2,32,1024]{2,1,0:T(8,128)(2,1)S(1)}, bf16[2,32,1024]{2,1,0:T(8,128)(2,1)S(1)}, u32[]{:S(2)}, u32[]{:S(2)}) collective-permute-start(bf16[2,32,1024]{2,1,0:T(8,128)(2,1)S(1)} %pad_maximum_fusion.2), channel_id=1, source_target_pairs={{0,8},{4,12},{8,0},{12,4},{16,24},{20,28},{24,16},{28,20},{1,9},{5... | collective-permute-start | bytes 393224 | tf_op jit(solution)/shard_map/ppermute | solution.py:29
  26.6 16.0 %collective-permute-start.2 = (bf16[4,32,1024]{2,1,0:T(8,128)(2,1)S(1)}, bf16[4,32,1024]{2,1,0:T(8,128)(2,1)S(1)}, u32[]{:S(2)}, u32[]{:S(2)}) collective-permute-start(bf16[4,32,1024]{2,1,0:T(8,128)(2,1)S(1)} %pad_maximum_fusion.1), channel_id=1, source_target_pairs={{0,16},{4,20},{8,24},{12,28},{16,0},{20,4},{24,8},{28,12},{1,17},{... | collective-permute-start | bytes 786440 | tf_op jit(solution)/shard_map/ppermute | solution.py:29
  47.3 2.0 %copy-start = (f32[16,8,64,128]{3,2,1,0:T(8,128)}, f32[16,8,64,128]{3,2,1,0:T(8,128)S(1)}, u32[]{:S(2)}) copy-start(f32[16,8,64,128]{3,2,1,0:T(8,128)S(1)} %get-tuple-element.36) | copy-start | bytes 12582916
  53.4 11.2 %all-to-all-start.2 = ((f32[8,1,256]{2,1,0:T(1,128)}), f32[8,1,256]{2,1,0:T(1,128)S(1)}, u32[]{:S(2)}, u32[]{:S(2)}) async-start(f32[8,1,256]{2,1,0:T(1,128)} %reshape.216), calls=%async_computation.2 | async-start | bytes 16384 | tf_op jit(solution)/shard_map/all_to_all | solution.py:105
  64.5 13.7 %all-to-all-start.1 = ((f32[8,1,256]{2,1,0:T(1,128)}), f32[8,1,256]{2,1,0:T(1,128)S(1)}, u32[]{:S(2)}, u32[]{:S(2)}) async-start(f32[8,1,256]{2,1,0:T(1,128)} %reshape.214), calls=%async_computation.1 | async-start | bytes 16384 | tf_op jit(solution)/shard_map/all_to_all | solution.py:104
  78.2 31.1 %all-to-all-start = ((f32[8,32,1024]{2,1,0:T(8,128)}), f32[8,32,1024]{2,1,0:T(8,128)S(1)}, u32[]{:S(2)}, u32[]{:S(2)}) async-start(f32[8,32,1024]{2,1,0:T(8,128)} %all_to_all.18), calls=%async_computation | async-start | bytes 2097152 | tf_op jit(solution)/shard_map/all_to_all | solution.py:106
  84.2 53.2 %reduce-scatter.2.cloned.1.call-start = ((), (), s32[]{:S(2)}) async-start(), calls=%async_computation.5 | async-start | bytes 655360 | tf_op jit(solution)/shard_map/reduce_scatter | solution.py:147
  110.8 5.9 %copy-start.4 = (s32[4,64]{1,0:T(4,128)S(1)}, s32[4,64]{1,0:T(4,128)}, u32[]{:S(2)}) copy-start(s32[4,64]{1,0:T(4,128)} %param.14) | copy-start | bytes 3076
  110.8 5.9 %copy-start.1 = (bf16[2,256,1024]{2,0,1:T(2,128)(2,1)S(1)}, bf16[2,256,1024]{2,0,1:T(2,128)(2,1)}, u32[]{:S(2)}) copy-start(bf16[2,256,1024]{2,0,1:T(2,128)(2,1)} %all-gather.2.cloned.1.call-done) | copy-start | bytes 3145732
Sparse Core Ops, SparseCore 0:
  12.1 47.1 all-gather.1
  116.8 20.5 reduce-scatter.1
